TPU v7x, 32 devices: a whole 2x2x4 slice. The times are simulated.
32 devices in a mesh: parts: 2 (over x), seq: 16 (over z, y, core).
Axes of the slice: x: 2, y: 2, z: 4, core: 2. Of those that a mesh axis runs over, the one named last changes fastest.
Arguments:
- control: bfloat16 [256, 3072], P(('parts', 'seq')), parts along dimension 0, may hold values from -6 to 6
- mask_ids: int32 [256], P(('parts', 'seq')), parts along dimension 0, may hold values from 0 to 2
- owner: int32 [256], P('parts'), parts along dimension 0, may hold values from 0 to 127, each once
- mask_table: bfloat16 [3, 3072], replicated, may hold values from -6 to 6
- res_weight: bfloat16 [3072, 3072], P(None, 'seq'), may hold values from -0.109375 to 0.109375
- base: bfloat16 [256, 3072], P(('parts', 'seq')), parts along dimension 0, may hold values from -6 to 6
- modulation: float32 [2, 3072], replicated, may hold values from -0.5 to 0.5
- q_weight: bfloat16 [3072, 1536], P(None, 'seq'), may hold values from -1 to 1
- k_weight: bfloat16 [3072, 1536], P(None, 'seq'), may hold values from -4 to 4
- v_weight: bfloat16 [3072, 1536], P(None, 'seq'), may hold values from -0.109375 to 0.109375
Outputs:
- hidden_out: bfloat16 [256, 3072], P(('parts', 'seq')), parts along dimension 0
- attended: bfloat16 [256, 1536], P(('parts', 'seq')), parts along dimension 0
There are 2 independent parts, one for each index of `parts`. A program takes and returns all parts, laid end to end along the dimension named above; an argument that names none is the same for every part. Nothing has to cross between parts.
Inputs may be any that keep to these rules, and one draw needn't show every extreme that they name: `owner`: each base row is named by exactly one control row.
All inputs are finite; a program needn't handle non-finite values.
Results may differ from a plain program's by a relative error of at most 0.006.
Values may be sent and summed in bfloat16 or wider, within the bound.
No kernel may reach another device: no remote copies, remote signals or barrier semaphores. Data moves between devices by JAX's collectives and lax.ppermute only.
A program may use at most 64 MiB of HBM per device.

v0:
```python
import math

import jax
import jax.numpy as jnp
from jax import lax
from jax.sharding import PartitionSpec as P

HEADS = 12
HEAD_DIM = 128


def layer_norm(hidden, modulation):
    row_mean = jnp.mean(hidden, axis=1, keepdims=True)
    centred = hidden - row_mean
    row_var = jnp.mean(centred * centred, axis=1, keepdims=True)
    scaled = centred * lax.rsqrt(row_var + 1e-06)
    return (scaled * (1.0 + modulation[1]) + modulation[0]).astype(jnp.bfloat16)


def attend_block(carried, segments, query_heads):
    running_max, running_sum, summed = carried
    key_rows, values = segments
    block_rows = key_rows.shape[0]
    key_heads = key_rows.reshape(block_rows, HEADS, HEAD_DIM)
    value_heads = values.reshape(block_rows, HEADS, HEAD_DIM)
    scores = jnp.einsum(
        "thd,khd->thk", query_heads, key_heads, preferred_element_type=jnp.float32
    ) / math.sqrt(HEAD_DIM)
    new_max = jnp.maximum(running_max, jnp.max(scores, axis=2))
    weights = jnp.exp(scores - new_max[:, :, None])
    running_sum = jnp.sum(weights, axis=2)
    summed = jnp.einsum(
        "thk,khd->thd",
        weights.astype(jnp.bfloat16),
        value_heads,
        preferred_element_type=jnp.float32,
    )
    return (new_max, running_sum, summed)


def on_device(
    control, mask_ids, owner, mask_table, res_weight, base, modulation, q_weight, k_weight, v_weight
):
    row_count = base.shape[0]
    selector = (
        mask_ids[:, None] == jnp.arange(mask_table.shape[0], dtype=jnp.int32)[None, :]
    ).astype(jnp.bfloat16)
    condition = (
        control.astype(jnp.float32)
        + jnp.dot(selector, mask_table, preferred_element_type=jnp.float32)
    ).astype(jnp.bfloat16)
    residual = jnp.dot(
        lax.all_gather(condition, "seq", axis=0, tiled=True),
        res_weight,
        preferred_element_type=jnp.float32,
    ).astype(jnp.bfloat16)
    total_rows = owner.shape[0]
    inverse = (
        jnp.zeros((total_rows,), jnp.int32).at[owner].set(jnp.arange(total_rows, dtype=jnp.int32))
    )
    relayed = lax.all_to_all(
        jnp.take(residual, inverse, axis=0), "seq", split_axis=0, concat_axis=1, tiled=True
    )
    hidden = base.astype(jnp.float32) + relayed.astype(jnp.float32)
    normed = layer_norm(hidden, modulation)
    joined = jnp.concatenate([q_weight, k_weight, v_weight], axis=1)
    col_width = q_weight.shape[1]
    columns = jnp.dot(
        lax.all_gather(normed, "seq", axis=0, tiled=True),
        joined,
        preferred_element_type=jnp.float32,
    ).astype(jnp.bfloat16)
    q_cols = columns[:, :col_width]
    k_cols = columns[:, col_width : 2 * col_width]
    v_cols = columns[:, 2 * col_width :]
    initial = (
        jnp.full((row_count, HEADS), -1e30, jnp.float32),
        jnp.zeros((row_count, HEADS), jnp.float32),
        jnp.zeros((row_count, HEADS, HEAD_DIM), jnp.float32),
    )
    queries = lax.all_to_all(q_cols, "seq", split_axis=0, concat_axis=1, tiled=True)
    key_rows, values = (
        lax.all_gather(k_cols, "seq", axis=1, tiled=True),
        lax.all_gather(v_cols, "seq", axis=1, tiled=True),
    )
    query_heads = queries.reshape(row_count, HEADS, HEAD_DIM)
    running_max, running_sum, summed = attend_block(initial, (key_rows, values), query_heads)
    attended = (
        (summed / running_sum[:, :, None]).reshape(row_count, HEADS * HEAD_DIM).astype(jnp.bfloat16)
    )
    return (hidden.astype(jnp.bfloat16), attended)


def solution(mesh):
    in_specs = (
        P(("parts", "seq"), None),
        P(("parts", "seq")),
        P("parts"),
        P(),
        P(None, "seq"),
        P(("parts", "seq"), None),
        P(),
        P(None, "seq"),
        P(None, "seq"),
        P(None, "seq"),
    )
    out_specs = (P(("parts", "seq"), None), P(("parts", "seq"), None))
    return jax.shard_map(
        on_device, mesh=mesh, in_specs=in_specs, out_specs=out_specs, check_vma=False
    )
```

profile of v0, /device:TPU:0, one launch (start us, length us, event | category | flops | bytes accessed | tf_op | source)
XLA Modules:
  0.0 110.4 jit_solution(8229619129411165652)
XLA Ops:
  0.6 0.8 compare_select_fusion.1
  1.4 1.0 scatter_custom_fusion
  2.5 1.0 fusion.1
  3.5 25.5 %all_gather.12 = bf16[128,3072]{1,0:T(8,128)(2,1)S(1)} all-gather(bf16[8,3072]{1,0:T(8,128)(2,1)S(1)} %fusion.1), channel_id=1, replica_groups=mesh['parts'=2,'seq'=16] {'seq'}, dimensions={0}, use_global_device_ids=true | all-gather | bytes 835584 | tf_op jit(solution)/shard_map/all_gather | solution.py:53
  29.0 0.5 convolution_convert_fusion
  29.5 0.1 copy.16
  29.7 0.8 gather_fusion
  30.5 0.7 bitcast_select_fusion
  31.2 3.5 %all-to-all-start = ((bf16[16,8,192]{2,1,0:T(8,128)(2,1)}), bf16[16,8,192]{2,1,0:T(8,128)(2,1)S(1)}, u32[]{:S(2)}, u32[]{:S(2)}) async-start(bf16[16,8,192]{2,1,0:T(8,128)(2,1)} %bitcast_select_fusion), calls=%async_computation | async-start | bytes 131072 | tf_op jit(solution)/shard_map/all_to_all | solution.py:61
  34.8 6.8 %all-to-all-done = bf16[16,8,192]{2,1,0:T(8,128)(2,1)S(1)} async-done(((bf16[16,8,192]{2,1,0:T(8,128)(2,1)}), bf16[16,8,192]{2,1,0:T(8,128)(2,1)S(1)}, u32[]{:S(2)}, u32[]{:S(2)}) %all-to-all-start) | async-done | bytes 49184 | tf_op jit(solution)/shard_map/all_to_all | solution.py:61
  41.7 0.1 reshape.55
  41.8 0.1 fusion.21
  41.9 0.2 multiply_reduce_fusion
  42.1 0.6 add_convert_fusion
  42.8 19.9 %all_gather.13 = bf16[128,3072]{1,0:T(8,128)(2,1)S(1)} all-gather(bf16[8,3072]{1,0:T(8,128)(2,1)S(1)} %get-tuple-element.2), channel_id=1, replica_groups=mesh['parts'=2,'seq'=16] {'seq'}, dimensions={0}, use_global_device_ids=true | all-gather | bytes 835584 | tf_op jit(solution)/shard_map/all_gather | solution.py:69
  62.7 0.6 fusion.8
  63.4 0.7 copy.18
  64.1 3.5 %all-to-all-start.1 = ((bf16[16,8,96]{2,1,0:T(8,128)(2,1)}), bf16[16,8,96]{2,1,0:T(8,128)(2,1)S(1)}, u32[]{:S(2)}, u32[]{:S(2)}) async-start(bf16[16,8,96]{2,1,0:T(8,128)(2,1)} %bitcast.6), calls=%async_computation.1 | async-start | bytes 65536 | tf_op jit(solution)/shard_map/all_to_all | solution.py:81
  67.6 22.7 %all_gather.15 = bf16[128,1536]{0,1:T(8,128)(2,1)S(1)} all-gather(bf16[128,96]{0,1:T(8,128)(2,1)S(1)} %get-tuple-element.5), channel_id=1, replica_groups=mesh['parts'=2,'seq'=16] {'seq'}, dimensions={1}, use_global_device_ids=true | all-gather | bytes 417792 | tf_op jit(solution)/shard_map/all_gather | solution.py:83
  90.3 18.5 %all_gather.14 = bf16[128,1536]{0,1:T(8,128)(2,1)S(1)} all-gather(bf16[128,96]{0,1:T(8,128)(2,1)S(1)} %get-tuple-element.6), channel_id=1, replica_groups=mesh['parts'=2,'seq'=16] {'seq'}, dimensions={1}, use_global_device_ids=true | all-gather | bytes 417792 | tf_op jit(solution)/shard_map/all_gather | solution.py:84
  108.8 0.1 reshape.54
  108.9 0.3 fusion.28
  109.2 0.4 convolution_bitcast_fusion
  109.6 0.8 fusion.14
  (26 shorter events, 0.3 us)
Async XLA Ops:
  0.6 28.4 %copy-start = (bf16[3072,192]{0,1:T(8,128)(2,1)S(1)}, bf16[3072,192]{0,1:T(8,128)(2,1)}, u32[]{:S(2)}) copy-start(bf16[3072,192]{0,1:T(8,128)(2,1)} %param.14) | copy-start | bytes 3538948
  29.0 5.7 %copy-start.2 = (f32[2,3072]{1,0:T(2,128)S(1)}, f32[2,3072]{1,0:T(2,128)}, u32[]{:S(2)}) copy-start(f32[2,3072]{1,0:T(2,128)} %param.16) | copy-start | bytes 73732
  29.5 12.2 %copy-start.1 = (bf16[8,3072]{1,0:T(8,128)(2,1)S(1)}, bf16[8,3072]{1,0:T(8,128)(2,1)}, u32[]{:S(2)}) copy-start(bf16[8,3072]{1,0:T(8,128)(2,1)} %param.15) | copy-start | bytes 147460
  30.5 32.2 %copy-start.3 = (bf16[3072,96]{0,1:T(8,128)(2,1)S(1)}, bf16[3072,96]{0,1:T(8,128)(2,1)}, u32[]{:S(2)}) copy-start(bf16[3072,96]{0,1:T(8,128)(2,1)} %param.19) | copy-start | bytes 1769476
  30.5 32.2 %copy-start.4 = (bf16[3072,96]{0,1:T(8,128)(2,1)S(1)}, bf16[3072,96]{0,1:T(8,128)(2,1)}, u32[]{:S(2)}) copy-start(bf16[3072,96]{0,1:T(8,128)(2,1)} %param.18) | copy-start | bytes 1769476
  30.5 32.2 %copy-start.5 = (bf16[3072,96]{0,1:T(8,128)(2,1)S(1)}, bf16[3072,96]{0,1:T(8,128)(2,1)}, u32[]{:S(2)}) copy-start(bf16[3072,96]{0,1:T(8,128)(2,1)} %param.17) | copy-start | bytes 1769476
  31.2 10.4 %all-to-all-start = ((bf16[16,8,192]{2,1,0:T(8,128)(2,1)}), bf16[16,8,192]{2,1,0:T(8,128)(2,1)S(1)}, u32[]{:S(2)}, u32[]{:S(2)}) async-start(bf16[16,8,192]{2,1,0:T(8,128)(2,1)} %bitcast_select_fusion), calls=%async_computation | async-start | bytes 131072 | tf_op jit(solution)/shard_map/all_to_all | solution.py:61
  64.1 44.7 %all-to-all-start.1 = ((bf16[16,8,96]{2,1,0:T(8,128)(2,1)}), bf16[16,8,96]{2,1,0:T(8,128)(2,1)S(1)}, u32[]{:S(2)}, u32[]{:S(2)}) async-start(bf16[16,8,96]{2,1,0:T(8,128)(2,1)} %bitcast.6), calls=%async_computation.1 | async-start | bytes 65536 | tf_op jit(solution)/shard_map/all_to_all | solution.py:81
where the time goes:
time: 111 us; the launch traced here: 110 us
  blocking collectives  86.6 us (78%)
  starting transfers between devices  6.97 us (6%)
  waiting for transfers between devices  6.82 us (6%)
  other arithmetic  3.32 us (3%)
  local copies, waits for them, and re-layouts  3.04 us (3%)
  matrix products  2.8 us (3%)
    all_gather x1, blocking collectives, on_device(): lax.all_gather(condition, 'seq', axis=0, tiled=True)  25.5 us
    all_gather x1, blocking collectives, on_device(): lax.all_gather(k_cols, 'seq', axis=1, tiled=True)  22.7 us
    all_gather x1, blocking collectives, on_device(): lax.all_gather(normed, 'seq', axis=0, tiled=True)  19.9 us
    all_gather x1, blocking collectives, on_device(): lax.all_gather(v_cols, 'seq', axis=1, tiled=True)  18.5 us
    all_to_all x1, waiting for transfers between devices, on_device(): lax.all_to_all(jnp.take(residual, inverse, axis=0), 'seq', split_axis=0,...  6.82 us
    all_to_all x1, starting transfers between devices, on_device(): lax.all_to_all(jnp.take(residual, inverse, axis=0), 'seq', split_axis=0,...  3.48 us
    all_to_all x1, starting transfers between devices, on_device(): lax.all_to_all(q_cols, 'seq', split_axis=0, concat_axis=1, tiled=True)  3.48 us
  transfers between devices with their start and end apart: 2, of which 1 were waited for; matrix products, arithmetic and copies ran while one was open for 0% of the time, Pallas kernels for 0%

commit v1 on v0

v1 whole, which is shorter than its diff:
```python
import functools
import math

import jax
import jax.numpy as jnp
from jax import lax
from jax.sharding import PartitionSpec as P

HEAD_DIM = 128


def ring_order(devices):
    chips = devices // 2
    narrow = 1
    while (2 * narrow) ** 2 <= chips and chips % (2 * narrow) == 0:
        narrow *= 2
    long = chips // narrow
    if narrow == 1:
        walk = [(row, 0) for row in range(long)]
    else:
        walk = [(row, 0) for row in range(long)]
        for back, row in enumerate(reversed(range(long))):
            columns = range(1, narrow) if back % 2 == 0 else range(narrow - 1, 0, -1)
            walk += [(row, column) for column in columns]
    return [(row * narrow + column) * 2 + core for row, column in walk for core in range(2)]


def layer_norm(hidden, modulation):
    row_mean = jnp.mean(hidden, axis=1, keepdims=True)
    centred = hidden - row_mean
    row_var = jnp.mean(centred * centred, axis=1, keepdims=True)
    scaled = centred * lax.rsqrt(row_var + 1e-06)
    return (scaled * (1.0 + modulation[1]) + modulation[0]).astype(jnp.bfloat16)


def on_device(
    devices,
    control,
    mask_ids,
    owner,
    mask_table,
    res_weight,
    base,
    modulation,
    q_weight,
    k_weight,
    v_weight,
):
    row_count = base.shape[0]
    total_rows = owner.shape[0]
    width = q_weight.shape[1]
    ring = ring_order(devices)
    team = math.lcm(width, HEAD_DIM) // width
    teams = devices // team
    team_heads = team * width // HEAD_DIM
    me = lax.axis_index("seq")
    place = me % team

    selector = (
        mask_ids[:, None] == jnp.arange(mask_table.shape[0], dtype=jnp.int32)[None, :]
    ).astype(jnp.bfloat16)
    condition = (
        control.astype(jnp.float32)
        + jnp.dot(selector, mask_table, preferred_element_type=jnp.float32)
    ).astype(jnp.bfloat16)
    conditions = lax.all_gather(condition, "seq", axis=0, tiled=True, axis_index_groups=[ring])
    residual = jnp.dot(conditions, res_weight, preferred_element_type=jnp.float32).astype(
        jnp.bfloat16
    )
    owner_ring = jnp.concatenate(
        [owner[place_ * row_count : (place_ + 1) * row_count] for place_ in ring]
    )
    relay = (jnp.arange(total_rows, dtype=jnp.int32)[:, None] == owner_ring[None, :]).astype(
        jnp.bfloat16
    )
    by_owner = jnp.dot(relay, residual, preferred_element_type=jnp.float32).astype(jnp.bfloat16)
    relayed = lax.all_to_all(by_owner, "seq", split_axis=0, concat_axis=1, tiled=True)
    hidden = base.astype(jnp.float32) + relayed.astype(jnp.float32)
    normed = layer_norm(hidden, modulation)
    joined = jnp.concatenate([q_weight, k_weight, v_weight], axis=1)
    normed_all = lax.all_gather(normed, "seq", axis=0, tiled=True, axis_index_groups=[ring])
    columns = lax.dot_general(
        joined, normed_all, (((0,), (1,)), ((), ())), preferred_element_type=jnp.float32
    ).astype(jnp.bfloat16)
    team_groups = [[t * team + r for r in range(team)] for t in range(teams)]
    columns = lax.all_gather(columns, "seq", axis=0, axis_index_groups=team_groups)
    columns = columns.reshape(team, 3, width, total_rows).transpose(1, 0, 2, 3)
    columns = columns.reshape(3, team_heads, HEAD_DIM, total_rows)
    spots = jnp.array([ring.index(d) for d in range(devices)], jnp.int32).reshape(teams, team)
    blocks = columns[0].reshape(team_heads, HEAD_DIM, devices, row_count)
    queries = jnp.take(blocks, jnp.take(spots, place, axis=1), axis=2)
    queries = queries.reshape(team_heads, HEAD_DIM, teams * row_count)
    scores = jnp.einsum(
        "hdt,hdk->htk", queries, columns[1], preferred_element_type=jnp.float32
    ) / math.sqrt(HEAD_DIM)
    expo = jnp.exp(scores - jnp.max(scores, axis=2, keepdims=True))
    denom = jnp.sum(expo, axis=2)
    summed = jnp.einsum(
        "htk,hdk->thd",
        expo.astype(jnp.bfloat16),
        columns[2],
        preferred_element_type=jnp.float32,
    )
    mine = (summed / denom.T[:, :, None]).astype(jnp.bfloat16)
    mine = mine.reshape(teams, row_count, team_heads * HEAD_DIM)
    place_groups = [[t * team + r for t in range(teams)] for r in range(team)]
    parts = lax.all_to_all(
        mine, "seq", split_axis=0, concat_axis=0, tiled=True, axis_index_groups=place_groups
    )
    attended = parts.transpose(1, 0, 2).reshape(row_count, teams * team_heads * HEAD_DIM)
    return (hidden.astype(jnp.bfloat16), attended)


def solution(mesh):
    in_specs = (
        P(("parts", "seq"), None),
        P(("parts", "seq")),
        P("parts"),
        P(),
        P(None, "seq"),
        P(("parts", "seq"), None),
        P(),
        P(None, "seq"),
        P(None, "seq"),
        P(None, "seq"),
    )
    out_specs = (P(("parts", "seq"), None), P(("parts", "seq"), None))
    return jax.shard_map(
        functools.partial(on_device, mesh.shape["seq"]),
        mesh=mesh,
        in_specs=in_specs,
        out_specs=out_specs,
        check_vma=False,
    )
```

time: 111 us -> 68.2 us (0.61)
  blocking collectives: 86.6 us -> 47.5 us
  starting transfers between devices: 6.97 us -> 3.93 us
  other arithmetic: 3.32 us -> 1.26 us
  local copies, waits for them, and re-layouts: 3.04 us -> 4.85 us
    all_gather x4 -> x3, blocking collectives: 86.6 us -> 38.3 us  [the longest x1 18 us: on_device(): lax.all_gather(condition, 'seq', axis=0, tiled=True, axis_index_groups=[r...]
    all_to_all x0 -> x1, blocking collectives: none -> 9.21 us  [on_device(): lax.all_to_all(mine, 'seq', split_axis=0, concat_axis=0, tiled=True, axis...]
    all_to_all x2 -> x1, starting transfers between devices: 6.97 us -> 3.93 us  [on_device(): lax.all_to_all(by_owner, 'seq', split_axis=0, concat_axis=1, tiled=True)]
    select_n x3 -> x1, other arithmetic: 1.46 us -> 0.01 us  [on_device(): queries = jnp.take(blocks, jnp.take(spots, place, axis=1), axis=2)]
    slice x2 -> x5, local copies, waits for them, and re-layouts: 0.73 us -> 2.07 us  [the longest x2 1.68 us: on_device(): owner[place_ * row_count:(place_ + 1) * row_count]]
    all_to_all x2 -> x1, waiting for transfers between devices: 6.82 us -> 6.61 us  [on_device(): lax.all_to_all(by_owner, 'seq', split_axis=0, concat_axis=1, tiled=True)]
  transfers between devices with their start and end apart: 2 -> 1, of which waited for: 1 -> 1; matrix products, arithmetic and copies ran while one was open for 0% -> 0% of each run, Pallas kernels for 0% -> 0%
where the time goes in v1:
time: 68.2 us; the launch traced here: 67.8 us
  blocking collectives  47.5 us (70%)
  waiting for transfers between devices  6.61 us (10%)
  local copies, waits for them, and re-layouts  4.85 us (7%)
  starting transfers between devices  3.93 us (6%)
  matrix products  2.82 us (4%)
  other arithmetic  1.26 us (2%)
  between operations  0.81 us (1%)
    all_gather x1, blocking collectives, on_device(): lax.all_gather(condition, 'seq', axis=0, tiled=True, axis_index_groups=[r...  18 us
    all_gather x1, blocking collectives, on_device(): lax.all_gather(normed, 'seq', axis=0, tiled=True, axis_index_groups=[ring])  14.2 us
    all_to_all x1, blocking collectives, on_device(): lax.all_to_all(mine, 'seq', split_axis=0, concat_axis=0, tiled=True, axis...  9.21 us
    all_to_all x1, waiting for transfers between devices, on_device(): lax.all_to_all(by_owner, 'seq', split_axis=0, concat_axis=1, tiled=True)  6.61 us
    all_gather x1, blocking collectives, on_device(): lax.all_gather(columns, 'seq', axis=0, axis_index_groups=team_groups)  6.11 us
    all_to_all x1, starting transfers between devices, on_device(): lax.all_to_all(by_owner, 'seq', split_axis=0, concat_axis=1, tiled=True)  3.93 us
    slice x2, local copies, waits for them, and re-layouts, on_device(): owner[place_ * row_count:(place_ + 1) * row_count]  1.68 us
  transfers between devices with their start and end apart: 1, of which 1 were waited for; matrix products, arithmetic and copies ran while one was open for 0% of the time, Pallas kernels for 0%

profile of v1, /device:TPU:0, one launch (start us, length us, event | category | flops | bytes accessed | tf_op | source)
XLA Modules:
  0.0 67.8 jit_solution(17814000194086659497)
XLA Ops:
  0.6 1.0 %fusion.27 = (s32[16]{0:T(128)S(1)}, s32[16]{0:T(128)S(1)}, s32[16]{0:T(128)S(1)}, s32[16]{0:T(128)S(1)}, s32[16]{0:T(128)S(1)}, /*index=5*/s32[16]{0:T(128)S(1)}) fusion(s32[128]{0:T(128)} %param.13), kind=kLoop, calls=%fused_computation.46 | loop fusion | bytes 768 | tf_op jit(solution)/shard_map/slice | solution.py:71
  1.6 0.7 %slice.58 = s32[32]{0:T(128)S(1)} slice(s32[128]{0:T(128)} %param.13), slice={[96:128]} | slice | bytes 256 | tf_op jit(solution)/shard_map/slice | solution.py:71
  2.3 1.0 %fusion = bf16[8,3072]{1,0:T(8,128)(2,1)S(1)} fusion(bf16[3,3072]{1,0:T(4,128)(2,1)} %param.14, bf16[8,3072]{1,0:T(8,128)(2,1)} %param.11, s32[8]{0:T(128)} %param.12), kind=kOutput, calls=%fused_computation.2 | convolution fusion | flops 221208 | bytes 116768 | tf_op jit(solution)/shard_map/dot_general | solution.py:64
  3.4 18.0 %all_gather.12 = bf16[128,3072]{1,0:T(8,128)(2,1)S(1)} all-gather(bf16[8,3072]{1,0:T(8,128)(2,1)S(1)} %fusion), channel_id=1, replica_groups={{0,1,4,5,8,9,12,13,14,15,10,11,6,7,2,3},{16,17,20,21,24,25,28,29,30,31,..., dimensions={0}, use_global_device_ids=true | all-gather | bytes 835584 | tf_op jit(solution)/shard_map/all_gather | solution.py:66
  21.5 0.7 convolution_convert_fusion
  22.1 0.7 %copy.20 = bf16[128,192]{1,0:T(8,128)(2,1)} copy(bf16[128,192]{0,1:T(8,128)(2,1)S(1)} %convolution_convert_fusion) | data formatting | bytes 98304 | tf_op jit(solution)/shard_map/convert_element_type | solution.py:76
  22.9 3.9 %all-to-all-start = ((bf16[16,8,192]{2,1,0:T(8,128)(2,1)}), bf16[16,8,192]{2,1,0:T(8,128)(2,1)S(1)}, u32[]{:S(2)}, u32[]{:S(2)}) async-start(bf16[16,8,192]{2,1,0:T(8,128)(2,1)} %bitcast), calls=%async_computation | async-start | bytes 131072 | tf_op jit(solution)/shard_map/all_to_all | solution.py:77
  27.1 6.6 %all-to-all-done = bf16[16,8,192]{2,1,0:T(8,128)(2,1)S(1)} async-done(((bf16[16,8,192]{2,1,0:T(8,128)(2,1)}), bf16[16,8,192]{2,1,0:T(8,128)(2,1)S(1)}, u32[]{:S(2)}, u32[]{:S(2)}) %all-to-all-start) | async-done | bytes 49184 | tf_op jit(solution)/shard_map/all_to_all | solution.py:77
  33.9 0.1 fusion.20
  34.0 0.2 multiply_reduce_fusion
  34.3 0.6 add_convert_fusion
  34.9 14.2 %all_gather.13 = bf16[128,3072]{1,0:T(8,128)(2,1)S(1)} all-gather(bf16[8,3072]{1,0:T(8,128)(2,1)S(1)} %get-tuple-element.16), channel_id=1, replica_groups={{0,1,4,5,8,9,12,13,14,15,10,11,6,7,2,3},{16,17,20,21,24,25,28,29,30,31,..., dimensions={0}, use_global_device_ids=true | all-gather | bytes 835584 | tf_op jit(solution)/shard_map/all_gather | solution.py:81
  49.1 0.6 fusion.7
  49.7 6.1 %all-gather = bf16[1152,128]{1,0:T(8,128)(2,1)S(1)} all-gather(bf16[288,128]{1,0:T(8,128)(2,1)S(1)} %fusion.7), channel_id=2, replica_groups={{0,1,2,3},{4,5,6,7},{8,9,10,11},{12,13,14,15},{16,17,18,19},{20,21,22,2..., dimensions={0}, use_global_device_ids=true | all-gather | bytes 368640 | tf_op jit(solution)/shard_map/all_gather | solution.py:86
  55.8 0.2 copy.22
  56.1 0.1 fusion.26
  56.4 0.1 copy.26
  56.5 0.1 reshape_squeeze.3
  56.7 0.6 gather_fusion
  57.2 0.3 fusion.28
  57.5 0.2 fusion.12
  57.7 0.2 fusion.11
  58.0 9.2 %all_to_all.18 = bf16[4,8,384]{2,1,0:T(8,128)(2,1)S(1)} all-to-all(bf16[4,8,384]{2,1,0:T(8,128)(2,1)S(1)} %reshape.74), channel_id=1, replica_groups={{0,4,8,12},{1,5,9,13},{2,6,10,14},{3,7,11,15},{16,20,24,28},{17,21,25,2..., dimensions={0} | all-to-all | bytes 49152 | tf_op jit(solution)/shard_map/all_to_all | solution.py:107
  67.2 0.6 copy.35
  (30 shorter events, 0.7 us)
Async XLA Ops:
  0.6 20.8 %copy-start = (bf16[3072,192]{0,1:T(8,128)(2,1)S(1)}, bf16[3072,192]{0,1:T(8,128)(2,1)}, u32[]{:S(2)}) copy-start(bf16[3072,192]{0,1:T(8,128)(2,1)} %param.15) | copy-start | bytes 3538948
  21.4 5.4 %copy-start.3 = (s32[4,4]{0,1:T(4,128)S(1)}, s32[4,4]{0,1:T(4,128)}, u32[]{:S(2)}) copy-start(s32[4,4]{0,1:T(4,128)} %constant.87) | copy-start | bytes 196
  21.4 5.5 %copy-start.2 = (f32[2,3072]{1,0:T(2,128)S(1)}, f32[2,3072]{1,0:T(2,128)}, u32[]{:S(2)}) copy-start(f32[2,3072]{1,0:T(2,128)} %param.17) | copy-start | bytes 73732
  21.5 12.4 %copy-start.1 = (bf16[8,3072]{1,0:T(8,128)(2,1)S(1)}, bf16[8,3072]{1,0:T(8,128)(2,1)}, u32[]{:S(2)}) copy-start(bf16[8,3072]{1,0:T(8,128)(2,1)} %param.16) | copy-start | bytes 147460
  22.9 26.2 %copy-start.4 = (bf16[3072,96]{0,1:T(8,128)(2,1)S(1)}, bf16[3072,96]{0,1:T(8,128)(2,1)}, u32[]{:S(2)}) copy-start(bf16[3072,96]{0,1:T(8,128)(2,1)} %param.20) | copy-start | bytes 1769476
  22.9 26.2 %copy-start.5 = (bf16[3072,96]{0,1:T(8,128)(2,1)S(1)}, bf16[3072,96]{0,1:T(8,128)(2,1)}, u32[]{:S(2)}) copy-start(bf16[3072,96]{0,1:T(8,128)(2,1)} %param.19) | copy-start | bytes 1769476
  22.9 26.2 %copy-start.6 = (bf16[3072,96]{0,1:T(8,128)(2,1)S(1)}, bf16[3072,96]{0,1:T(8,128)(2,1)}, u32[]{:S(2)}) copy-start(bf16[3072,96]{0,1:T(8,128)(2,1)} %param.18) | copy-start | bytes 1769476
  22.9 10.8 %all-to-all-start = ((bf16[16,8,192]{2,1,0:T(8,128)(2,1)}), bf16[16,8,192]{2,1,0:T(8,128)(2,1)S(1)}, u32[]{:S(2)}, u32[]{:S(2)}) async-start(bf16[16,8,192]{2,1,0:T(8,128)(2,1)} %bitcast), calls=%async_computation | async-start | bytes 131072 | tf_op jit(solution)/shard_map/all_to_all | solution.py:77

commit v2 on v1

--- a/solution.py
+++ b/solution.py
@@ -4,6 +4,8 @@
 import jax
 import jax.numpy as jnp
 from jax import lax
+from jax.experimental import pallas as pl
+from jax.experimental.pallas import tpu as pltpu
 from jax.sharding import PartitionSpec as P
 
 HEAD_DIM = 128
@@ -33,7 +35,7 @@
     return (scaled * (1.0 + modulation[1]) + modulation[0]).astype(jnp.bfloat16)
 
 
-def on_device(
+def on_device_plain(
     devices,
     control,
     mask_ids,
@@ -111,6 +113,280 @@
     return (hidden.astype(jnp.bfloat16), attended)
 
 
+VMEM = pl.BlockSpec(memory_space=pltpu.VMEM)
+SMEM = pl.BlockSpec(memory_space=pltpu.SMEM)
+HBM = pl.BlockSpec(memory_space=pltpu.HBM)
+NT = (((1,), (1,)), ((), ()))
+STAT_ROWS = 16
+
+
+def call(kernel, out_shape, in_specs, scratch=(), limit=8 << 20):
+    multiple = isinstance(out_shape, (tuple, list))
+    return pl.pallas_call(
+        kernel,
+        out_shape=out_shape,
+        in_specs=in_specs,
+        out_specs=[VMEM] * len(out_shape) if multiple else VMEM,
+        scratch_shapes=list(scratch),
+        compiler_params=pltpu.CompilerParams(vmem_limit_bytes=limit),
+    )
+
+
+def matmul_nt(left, right):
+    return lax.dot_general(left, right, NT, preferred_element_type=jnp.float32)
+
+
+def identity(size):
+    rows = lax.broadcasted_iota(jnp.int32, (size, size), 0)
+    return (rows == lax.broadcasted_iota(jnp.int32, (size, size), 1)).astype(jnp.bfloat16)
+
+
+def condition_kernel(
+    far_ids,
+    far_control,
+    far_table,
+    far_base,
+    far_weight,
+    far_owner,
+    condition,
+    pieces,
+    weight,
+    owner,
+    ids,
+    control,
+    table,
+    base,
+    arrived,
+):
+    copies = [
+        pltpu.make_async_copy(source, target, arrived.at[i])
+        for i, (source, target) in enumerate(
+            (
+                (far_base, base),
+                (far_ids, ids),
+                (far_table, table),
+                (far_control, control),
+                (far_owner, owner),
+                (far_weight, weight),
+            )
+        )
+    ]
+    for copy in copies:
+        copy.start()
+    rows, model = control.shape
+    kinds = table.shape[0]
+    devices, _, block = pieces.shape
+    copies[0].wait()
+    for d in range(devices):
+        pieces[d] = base[:, d * block : (d + 1) * block]
+    copies[1].wait()
+    kind = jnp.zeros((rows, 1), jnp.int32)
+    row = lax.broadcasted_iota(jnp.int32, (rows, 1), 0)
+    for i in range(rows):
+        kind = jnp.where(row == i, ids[i], kind)
+    copies[2].wait()
+    copies[3].wait()
+    entries = table[...].astype(jnp.float32)
+    chosen = jnp.broadcast_to(entries[:1], (rows, model))
+    for j in range(1, kinds):
+        chosen = jnp.where(kind == j, entries[j : j + 1], chosen)
+    condition[...] = (control[...].astype(jnp.float32) + chosen).astype(jnp.bfloat16)
+    copies[4].wait()
+    copies[5].wait()
+
+
+def residual_kernel(ring, conditions, weight, owner, base, out):
+    rows = conditions.shape[0]
+    block = weight.shape[0]
+    count = rows // len(ring)
+    residual = matmul_nt(weight[...], conditions[...]).astype(jnp.bfloat16)
+    row = lax.broadcasted_iota(jnp.int32, (rows, rows), 0)
+    names = (row == owner[...]).astype(jnp.bfloat16)
+    lane = lax.broadcasted_iota(jnp.int32, (1, rows), 1)
+    holder = jnp.zeros((1, rows), jnp.int32)
+    for s, device in enumerate(ring):
+        holder = jnp.where(lane // count == s, device, holder)
+    turned = (row == holder * count + lane % count).astype(jnp.bfloat16)
+    relay = jnp.dot(names, turned, preferred_element_type=jnp.float32).astype(jnp.bfloat16)
+    own = base[...].astype(jnp.float32).reshape(rows, block).astype(jnp.bfloat16)
+    hidden = matmul_nt(residual, relay) + matmul_nt(identity(block), own)
+    middle = jnp.mean(hidden, axis=0, keepdims=True)
+    apart = hidden - middle
+    squares = jnp.sum(apart * apart, axis=0, keepdims=True)
+    out[:block] = apart.astype(jnp.bfloat16)
+    line = lax.broadcasted_iota(jnp.int32, (STAT_ROWS, rows), 0)
+    stats = jnp.zeros((STAT_ROWS, rows), jnp.float32)
+    for first, value in ((0, middle), (3, squares)):
+        for term in range(3):
+            head = value.astype(jnp.bfloat16).astype(jnp.float32)
+            stats = jnp.where(line == first + term, head, stats)
+            value = value - head
+    out[block:] = stats.astype(jnp.bfloat16)
+
+
+def project_kernel(
+    ring, me, gathered, modulation, q_weight, k_weight, v_weight, columns, hidden_out, normed, turned
+):
+    devices = len(ring)
+    rows = gathered.shape[1]
+    stride = gathered.shape[0] // devices
+    block = stride - STAT_ROWS
+    model = block * devices
+    count = hidden_out.shape[0]
+    width = q_weight.shape[0]
+    middles, squares = [], jnp.zeros((1, rows), jnp.float32)
+    for s in range(devices):
+        stats = gathered[s * stride + block : (s + 1) * stride].astype(jnp.float32)
+        middles.append(stats[0:1] + stats[1:2] + stats[2:3])
+        squares = squares + (stats[3:4] + stats[4:5] + stats[5:6])
+    mean = sum(middles) * (1.0 / devices)
+    offsets = [middle - mean for middle in middles]
+    for offset in offsets:
+        squares = squares + block * (offset * offset)
+    inverse = lax.rsqrt(squares * (1.0 / model) + 1e-06)
+    table = jnp.concatenate(
+        offsets + [inverse, mean, jnp.zeros((rows - devices - 2, rows), jnp.float32)], axis=0
+    )
+    turned[...] = table.T
+    inverse_column = turned[:, devices : devices + 1]
+    first = pl.multiple_of(me[0] * count, count)
+    mine = turned[pl.ds(first, count), :]
+    eye = identity(rows)
+    own_row = lax.broadcasted_iota(jnp.int32, (count, rows), 0) + first
+    pick = (own_row == lax.broadcasted_iota(jnp.int32, (count, rows), 1)).astype(jnp.bfloat16)
+    pair = 2 * block
+    side = lax.broadcasted_iota(jnp.int32, (1, pair), 1) < block
+    for p in range(devices // 2):
+        lanes = slice(ring[2 * p] * block, ring[2 * p] * block + pair)
+        start = 2 * p * stride
+        apart = jnp.concatenate(
+            [gathered[start : start + block], gathered[start + stride : start + stride + block]],
+            axis=0,
+        )
+        centred = matmul_nt(eye, apart) + jnp.where(
+            side, turned[:, 2 * p : 2 * p + 1], turned[:, 2 * p + 1 : 2 * p + 2]
+        )
+        scaled = (centred * inverse_column) * (1.0 + modulation[1:2, lanes])
+        normed[:, lanes] = (scaled + modulation[0:1, lanes]).astype(jnp.bfloat16)
+        own = matmul_nt(pick, apart) + jnp.where(
+            side, mine[:, 2 * p : 2 * p + 1], mine[:, 2 * p + 1 : 2 * p + 2]
+        )
+        hidden_out[:, lanes] = (own + mine[:, devices + 1 : devices + 2]).astype(jnp.bfloat16)
+    for j, weight in enumerate((q_weight, k_weight, v_weight)):
+        columns[j * width : (j + 1) * width] = matmul_nt(weight[...], normed[...]).astype(
+            jnp.bfloat16
+        )
+
+
+def attend_kernel(place, gathered, out, queries, keys, values):
+    team, tall, rows = gathered.shape
+    width = tall // 3
+    teams, count, _ = out.shape
+    for r in range(team):
+        span = slice(r * width, (r + 1) * width)
+        queries[span] = gathered[r, :width]
+        keys[span] = gathered[r, width : 2 * width]
+        values[span] = gathered[r, 2 * width :]
+    line = lax.broadcasted_iota(jnp.int32, (teams * count, rows), 0)
+    wanted = ((line // count) * team + place[0]) * count + line % count
+    pick = (wanted == lax.broadcasted_iota(jnp.int32, (teams * count, rows), 1)).astype(
+        jnp.bfloat16
+    )
+    chosen = matmul_nt(pick, queries[...]).astype(jnp.bfloat16)
+    for h in range(team * width // HEAD_DIM):
+        span = slice(h * HEAD_DIM, (h + 1) * HEAD_DIM)
+        scores = jnp.dot(
+            chosen[:, span], keys[span], preferred_element_type=jnp.float32
+        ) / math.sqrt(HEAD_DIM)
+        expo = jnp.exp(scores - jnp.max(scores, axis=1, keepdims=True))
+        denom = jnp.sum(expo, axis=1, keepdims=True)
+        mixed = matmul_nt(expo.astype(jnp.bfloat16), values[span]) / denom
+        out[:, :, span] = mixed.reshape(teams, count, HEAD_DIM).astype(jnp.bfloat16)
+
+
+def on_device(
+    devices,
+    control,
+    mask_ids,
+    owner,
+    mask_table,
+    res_weight,
+    base,
+    modulation,
+    q_weight,
+    k_weight,
+    v_weight,
+):
+    count, model = base.shape
+    rows = owner.shape[0]
+    block = res_weight.shape[1]
+    width = q_weight.shape[1]
+    ring = ring_order(devices)
+    team = math.lcm(width, HEAD_DIM) // width
+    teams = devices // team
+    me = lax.axis_index("seq")
+    bf16 = jnp.bfloat16
+    shape = jax.ShapeDtypeStruct
+
+    inputs = (mask_ids, control, mask_table, base, res_weight.T, owner.reshape(1, rows))
+    condition, pieces, near_weight, near_owner = call(
+        condition_kernel,
+        (
+            pltpu.VMEM((count, model), bf16),
+            pltpu.HBM((devices, count, block), bf16),
+            pltpu.VMEM((block, model), bf16),
+            pltpu.VMEM((1, rows), jnp.int32),
+        ),
+        [HBM] * len(inputs),
+        [
+            pltpu.SMEM((count,), jnp.int32),
+            pltpu.VMEM((count, model), bf16),
+            pltpu.VMEM(mask_table.shape, bf16),
+            pltpu.VMEM((count, model), bf16),
+            pltpu.SemaphoreType.DMA((len(inputs),)),
+        ],
+    )(*[pltpu.with_memory_space_constraint(x, pltpu.HBM) for x in inputs])
+    base_columns = lax.all_to_all(pieces, "seq", split_axis=0, concat_axis=0, tiled=True)
+    conditions = lax.all_gather(condition, "seq", axis=0, tiled=True, axis_index_groups=[ring])
+    payload = call(
+        functools.partial(residual_kernel, ring),
+        shape((block + STAT_ROWS, rows), bf16),
+        [VMEM] * 4,
+    )(conditions, near_weight, near_owner, base_columns)
+    gathered = lax.all_gather(payload, "seq", axis=0, tiled=True, axis_index_groups=[ring])
+    columns, hidden_out = call(
+        functools.partial(project_kernel, ring),
+        (shape((3 * width, rows), bf16), shape((count, model), bf16)),
+        [SMEM] + [VMEM] * 5,
+        [pltpu.VMEM((rows, model), bf16), pltpu.VMEM((rows, rows), jnp.float32)],
+    )(me.reshape(1), gathered, modulation, q_weight.T, k_weight.T, v_weight.T)
+    team_groups = [[t * team + r for r in range(team)] for t in range(teams)]
+    columns = lax.all_gather(columns, "seq", axis=0, axis_index_groups=team_groups)
+    head_columns = team * width
+    mine = call(
+        attend_kernel,
+        shape((teams, count, head_columns), bf16),
+        [SMEM, VMEM],
+        [pltpu.VMEM((head_columns, rows), bf16)] * 3,
+    )((me % team).reshape(1), columns)
+    place_groups = [[t * team + r for t in range(teams)] for r in range(team)]
+    parts = lax.all_to_all(
+        mine, "seq", split_axis=0, concat_axis=0, tiled=True, axis_index_groups=place_groups
+    )
+    attended = parts.transpose(1, 0, 2).reshape(count, teams * head_columns)
+    return (hidden_out, attended)
+
+
+def fits(devices, rows, block, width):
+    return rows == HEAD_DIM and devices % 2 == 0 and block % 64 == 0 and width % 16 == 0
+
+
+def on_any_device(devices, *arguments):
+    owner, res_weight, q_weight = arguments[2], arguments[4], arguments[7]
+    tidy = fits(devices, owner.shape[0], res_weight.shape[1], q_weight.shape[1])
+    return (on_device if tidy else on_device_plain)(devices, *arguments)
+
+
 def solution(mesh):
     in_specs = (
         P(("parts", "seq"), None),
@@ -126,7 +402,7 @@
     )
     out_specs = (P(("parts", "seq"), None), P(("parts", "seq"), None))
     return jax.shard_map(
-        functools.partial(on_device, mesh.shape["seq"]),
+        functools.partial(on_any_device, mesh.shape["seq"]),
         mesh=mesh,
         in_specs=in_specs,
         out_specs=out_specs,

time: 68.2 us -> 60.9 us (0.89)
  waiting for transfers between devices: 6.61 us -> 0.01 us
  Pallas kernels: 0 us -> 5.47 us
  local copies, waits for them, and re-layouts: 4.85 us -> 0.63 us
  starting transfers between devices: 3.93 us -> 7.43 us
  matrix products: 2.82 us -> 0 us
  other arithmetic: 1.26 us -> 0 us
  blocking collectives: 47.5 us -> 46.5 us
    all_to_all x1, waiting for transfers between devices: 6.61 us -> 0.01 us  [on_device(): lax.all_to_all(pieces, 'seq', split_axis=0, concat_axis=0, tiled=True)]
    pallas_call x0 -> x4, Pallas kernels: none -> 5.47 us  [the longest x1 2.03 us: on_device(): call(condition_kernel, (pltpu.VMEM((count, model), bf16), pltpu.HBM((devi...]
    all_to_all x1, starting transfers between devices: 3.93 us -> 7.43 us  [on_device(): lax.all_to_all(pieces, 'seq', split_axis=0, concat_axis=0, tiled=True)]
    dot_general x5 -> x0, matrix products: 2.82 us -> none  [the longest x1 1.03 us: on_device(): jnp.dot(selector, mask_table, preferred_element_type=jnp.float32)]
    slice x5 -> x0, local copies, waits for them, and re-layouts: 2.07 us -> none  [the longest x2 1.68 us: on_device(): owner[place_ * row_count:(place_ + 1) * row_count]]
    all_gather x1, blocking collectives: 18 us -> 16.8 us  [on_device(): lax.all_gather(condition, 'seq', axis=0, tiled=True, axis_index_groups=[r...]
    all_gather x1, blocking collectives: 14.2 us -> 15.4 us  [on_device(): lax.all_gather(payload, 'seq', axis=0, tiled=True, axis_index_groups=[ring])]
    all_to_all x1, blocking collectives: 9.21 us -> 8.25 us  [on_device(): lax.all_to_all(mine, 'seq', split_axis=0, concat_axis=0, tiled=True, axis...]
  transfers between devices with their start and end apart: 1 -> 1, of which waited for: 1 -> 0; matrix products, arithmetic and copies ran while one was open for 0% -> 0% of each run, Pallas kernels for 0% -> 0%
where the time goes in v2:
time: 60.9 us; the launch traced here: 60.6 us
  blocking collectives  46.5 us (76%)
  starting transfers between devices  7.43 us (12%)
  Pallas kernels  5.47 us (9%)
  between operations  0.67 us (1%)
  local copies, waits for them, and re-layouts  0.63 us (1%)
    all_gather x1, blocking collectives, on_device(): lax.all_gather(condition, 'seq', axis=0, tiled=True, axis_index_groups=[r...  16.8 us
    all_gather x1, blocking collectives, on_device(): lax.all_gather(payload, 'seq', axis=0, tiled=True, axis_index_groups=[ring])  15.4 us
    all_to_all x1, blocking collectives, on_device(): lax.all_to_all(mine, 'seq', split_axis=0, concat_axis=0, tiled=True, axis...  8.25 us
    all_to_all x1, starting transfers between devices, on_device(): lax.all_to_all(pieces, 'seq', split_axis=0, concat_axis=0, tiled=True)  7.43 us
    all_gather x1, blocking collectives, on_device(): lax.all_gather(columns, 'seq', axis=0, axis_index_groups=team_groups)  6.03 us
    pallas_call x1, Pallas kernels, on_device(): call(condition_kernel, (pltpu.VMEM((count, model), bf16), pltpu.HBM((devi...  2.03 us
    pallas_call x1, Pallas kernels, on_device(): call(functools.partial(project_kernel, ring), (shape((3 * width, rows), b...  2.02 us
  transfers between devices with their start and end apart: 1, of which 0 were waited for; matrix products, arithmetic and copies ran while one was open for 0% of the time, Pallas kernels for 0%

profile of v2, /device:TPU:0, one launch (start us, length us, event | category | flops | bytes accessed | tf_op | source)
XLA Modules:
  0.0 60.6 jit_solution(9816694218582176107)
XLA Ops:
  0.6 2.0 %shard_map.113 = (bf16[8,3072]{1,0:T(8,128)(2,1)S(1)}, bf16[16,8,192]{2,1,0:T(8,128)(2,1)}, bf16[192,3072]{1,0:T(8,128)(2,1)S(1)}, s32[1,128]{1,0:T(1,128)S(1)}) custom-call(s32[8]{0:T(128)} %far_ids.1, bf16[8,3072]{1,0:T(8,128)(2,1)} %far_control.1, bf16[3,3072]{1,0:T(4,128)(2,1)} %far_table.1, bf16[8,3072]{1,0:T(8,128)(2,1)} %far_base.1, ...), custom_call_target="tpu_custom_call" | custom-call | tf_op jit(solution)/shard_map/pallas_call | solution.py:332
  2.7 7.4 %all-to-all-start = ((bf16[16,8,192]{2,1,0:T(8,128)(2,1)}), bf16[16,8,192]{2,1,0:T(8,128)(2,1)S(1)}, u32[]{:S(2)}, u32[]{:S(2)}) async-start(bf16[16,8,192]{2,1,0:T(8,128)(2,1)} %get-tuple-element.11), calls=%async_computation | async-start | bytes 131072 | tf_op jit(solution)/shard_map/all_to_all | solution.py:349
  10.1 16.8 %all_gather.12.conditions = bf16[128,3072]{1,0:T(8,128)(2,1)S(1)} all-gather(bf16[8,3072]{1,0:T(8,128)(2,1)S(1)} %get-tuple-element.8), channel_id=1, replica_groups={{0,1,4,5,8,9,12,13,14,15,10,11,6,7,2,3},{16,17,20,21,24,25,28,29,30,31,..., dimensions={0}, use_global_device_ids=true | all-gather | bytes 835584 | tf_op jit(solution)/shard_map/all_gather | solution.py:350
  26.9 0.0 all-to-all-done.base
  26.9 0.0 copy-start
  26.9 0.0 copy-start.1
  26.9 0.0 copy-start.2
  26.9 0.0 copy-start.3
  26.9 0.7 %shard_map.114 = bf16[208,128]{1,0:T(8,128)(2,1)S(1)} custom-call(bf16[128,3072]{1,0:T(8,128)(2,1)S(1)} %all_gather.12.conditions, bf16[192,3072]{1,0:T(8,128)(2,1)S(1)} %get-tuple-element.9.weight, s32[1,128]{1,0:T(1,128)S(1)} %get-tuple-element.10.owner, bf16[16,8,192]{2,1,0:T(8,128)(2,1)S(1)} %all-to-all-done.base), custom_call_target="tpu_custom_call" | custom-call | tf_op jit(solution)/shard_map/pallas_call | solution.py:351
  27.6 15.4 %all_gather.13.gathered = bf16[3328,128]{1,0:T(8,128)(2,1)S(1)} all-gather(bf16[208,128]{1,0:T(8,128)(2,1)S(1)} %shard_map.114), channel_id=1, replica_groups={{0,1,4,5,8,9,12,13,14,15,10,11,6,7,2,3},{16,17,20,21,24,25,28,29,30,31,..., dimensions={0}, use_global_device_ids=true | all-gather | bytes 905216 | tf_op jit(solution)/shard_map/all_gather | solution.py:356
  43.0 0.0 copy-done
  43.0 0.0 copy-done.1
  43.0 0.0 copy-done.2
  43.0 0.0 copy-done.3
  43.0 2.0 %shard_map.115 = (bf16[288,128]{1,0:T(8,128)(2,1)S(1)}, bf16[8,3072]{1,0:T(8,128)(2,1)}) custom-call(s32[1]{0:T(128)} %bitcast.me, bf16[3328,128]{1,0:T(8,128)(2,1)S(1)} %all_gather.13.gathered, f32[2,3072]{1,0:T(2,128)S(1)} %copy-done.3, bf16[96,3072]{1,0:T(8,128)(2,1)S(1)} %bitcast.12, bf16[96,3072]{1,0:T(8,128)(2,1)S(1)} %bitcast.13, ...), custom_call_target="tpu_custom_call" | custom-call | tf_op jit(solution)/shard_map/pallas_call | solution.py:357
  45.1 6.0 %all-gather = bf16[1152,128]{1,0:T(8,128)(2,1)S(1)} all-gather(bf16[288,128]{1,0:T(8,128)(2,1)S(1)} %get-tuple-element.13), channel_id=2, replica_groups={{0,1,2,3},{4,5,6,7},{8,9,10,11},{12,13,14,15},{16,17,18,19},{20,21,22,2..., dimensions={0}, use_global_device_ids=true | all-gather | bytes 368640 | tf_op jit(solution)/shard_map/all_gather | solution.py:364
  51.1 0.7 %shard_map.116 = bf16[4,8,384]{2,1,0:T(8,128)(2,1)S(1)} custom-call(s32[1]{0:T(128)} %bitcast.6.place, bf16[4,288,128]{2,1,0:T(8,128)(2,1)S(1)} %bitcast.11), custom_call_target="tpu_custom_call" | custom-call | tf_op jit(solution)/shard_map/pallas_call | solution.py:366
  51.8 8.3 %all_to_all.10 = bf16[4,8,384]{2,1,0:T(8,128)(2,1)S(1)} all-to-all(bf16[4,8,384]{2,1,0:T(8,128)(2,1)S(1)} %shard_map.116), channel_id=1, replica_groups={{0,4,8,12},{1,5,9,13},{2,6,10,14},{3,7,11,15},{16,20,24,28},{17,21,25,2..., dimensions={0} | all-to-all | bytes 49152 | tf_op jit(solution)/shard_map/all_to_all | solution.py:373
  60.0 0.6 %copy.13 = bf16[8,1536]{1,0:T(8,128)(2,1)} copy(bf16[8,1536]{1,0:T(8,128)(2,1)S(1)} %bitcast.16) | data formatting | bytes 49152
Async XLA Ops:
  2.7 24.2 %all-to-all-start = ((bf16[16,8,192]{2,1,0:T(8,128)(2,1)}), bf16[16,8,192]{2,1,0:T(8,128)(2,1)S(1)}, u32[]{:S(2)}, u32[]{:S(2)}) async-start(bf16[16,8,192]{2,1,0:T(8,128)(2,1)} %get-tuple-element.11), calls=%async_computation | async-start | bytes 131072 | tf_op jit(solution)/shard_map/all_to_all | solution.py:349
  26.9 16.2 %copy-start = (bf16[3072,96]{0,1:T(8,128)(2,1)S(1)}, bf16[3072,96]{0,1:T(8,128)(2,1)}, u32[]{:S(2)}) copy-start(bf16[3072,96]{0,1:T(8,128)(2,1)} %param.17) | copy-start | bytes 1769476
  26.9 16.2 %copy-start.1 = (bf16[3072,96]{0,1:T(8,128)(2,1)S(1)}, bf16[3072,96]{0,1:T(8,128)(2,1)}, u32[]{:S(2)}) copy-start(bf16[3072,96]{0,1:T(8,128)(2,1)} %param.18) | copy-start | bytes 1769476
  26.9 16.2 %copy-start.2 = (bf16[3072,96]{0,1:T(8,128)(2,1)S(1)}, bf16[3072,96]{0,1:T(8,128)(2,1)}, u32[]{:S(2)}) copy-start(bf16[3072,96]{0,1:T(8,128)(2,1)} %param.19) | copy-start | bytes 1769476
  26.9 16.2 %copy-start.3 = (f32[2,3072]{1,0:T(2,128)S(1)}, f32[2,3072]{1,0:T(2,128)}, u32[]{:S(2)}) copy-start(f32[2,3072]{1,0:T(2,128)} %modulation.1) | copy-start | bytes 73732
